TPU v7x, 512 devices: a whole 4x4x16 slice. The times are simulated.
512 devices in a mesh: slab: 64 (over z, x_hi, core), band: 8 (over y, x_lo).
Axes of the slice: x: 4 (x_hi: 2, x_lo: 2; x = x_hi * 2 + x_lo), y: 4, z: 16, core: 2. Of those that a mesh axis runs over, the one named last changes fastest.
Arguments:
- hamiltonian: bfloat16 [512, 7, 128, 128], P('slab', None, 'band'), may hold values from -0.1875 to 0.1875
- neighbors: int32 [512, 7], P('slab'), may hold values from 0 to 11, as said below
- orbitals: bfloat16 [65536, 1024], P('slab', 'band'), may hold values from -6 to 6
Outputs:
- residual: bfloat16 [65536, 1024], P(('slab', 'band'))
Inputs may be any that keep to these rules, and one draw needn't show every extreme that they name: `neighbors`: window positions 0 to 1 are the last 2 elements of the slab below (periodic), 2 to 9 the slab's own elements, the rest the first 2 elements of the slab above. A slab's elements are in layers of 2; each block row names, in an order of its own, itself, the element 2 positions below and above it in the window, and four elements of its own layer (repeats possible).
All inputs are finite; a program needn't handle non-finite values.
Results may differ from a plain program's by a relative error of at most 0.012.
Values may be sent and summed in bfloat16 or wider, within the bound.
No kernel may reach another device: no remote copies, remote signals or barrier semaphores. Data moves between devices by JAX's collectives and lax.ppermute only.
A program may use at most 64 MiB of HBM per device.

v0:
```python
import math
import jax
import jax.numpy as jnp
from jax import lax
from jax.sharding import PartitionSpec as P

FACE = 2


def padded(block, sides, width):
    for axis, dim in sides:
        count = lax.axis_size(axis)
        forward = [(i, i + 1) for i in range(count - 1)]
        forward.append((count - 1, 0))
        backward = [(target, source) for source, target in forward]
        low = lax.ppermute(
            lax.slice_in_dim(block, block.shape[dim] - width, None, axis=dim), axis, forward
        )
        high = lax.ppermute(lax.slice_in_dim(block, 0, width, axis=dim), axis, backward)
        block = jnp.concatenate([low, block, high], axis=dim)
    return block


def apply_local(vector, full_tiles, neighbors):
    tile_size = full_tiles.shape[2]
    extended = padded(vector, (("slab", 0),), FACE * tile_size)
    blocks = extended.reshape(-1, tile_size, vector.shape[1])
    picked_blocks = blocks[neighbors]
    product = jnp.einsum(
        "rjab,rjbc->rac", full_tiles, picked_blocks, preferred_element_type=jnp.float32
    )
    return product.reshape(vector.shape[0], vector.shape[1])


def body(hamiltonian, neighbors, orbitals):
    full_tiles = lax.all_gather(hamiltonian, "band", axis=2, tiled=True)
    first = apply_local(orbitals, full_tiles, neighbors).astype(jnp.bfloat16)
    second = (
        2.0 * apply_local(first, full_tiles, neighbors) - orbitals.astype(jnp.float32)
    ).astype(jnp.bfloat16)
    third = (2.0 * apply_local(second, full_tiles, neighbors) - first.astype(jnp.float32)).astype(
        jnp.bfloat16
    )
    applied = apply_local(third, full_tiles, neighbors).astype(jnp.bfloat16)
    rows_all = orbitals.shape[0] * lax.axis_size("slab")
    bands_all = orbitals.shape[1] * lax.axis_size("band")
    gram_scale = 1.0 / math.sqrt(float(rows_all) * float(bands_all))
    strip_third, strip_applied = (
        lax.all_to_all(third, "band", split_axis=0, concat_axis=1, tiled=True),
        lax.all_to_all(applied, "band", split_axis=0, concat_axis=1, tiled=True),
    )
    partial_value = jnp.einsum(
        "rb,rc->bc", strip_third, strip_applied, preferred_element_type=jnp.float32
    )
    summed = lax.psum(partial_value, ("slab", "band"))
    gram_full = (summed * gram_scale).astype(jnp.bfloat16)
    mixed = jnp.dot(strip_third, gram_full, preferred_element_type=jnp.float32)
    return (strip_applied.astype(jnp.float32) - mixed).astype(jnp.bfloat16)


def solution(mesh):
    in_specs = (P("slab", None, "band", None), P("slab", None), P("slab", "band"))
    out_specs = P(("slab", "band"), None)
    return jax.shard_map(body, mesh=mesh, in_specs=in_specs, out_specs=out_specs, check_vma=False)
```

profile of v0, /device:TPU:2, one launch (start us, length us, event | category | flops | bytes accessed | tf_op | source)
XLA Modules:
  0.0 640.3 jit_solution(16940214057220224389)
XLA Ops:
  6.5 0.0 all-gather.2.cloned.1.call-start
  6.5 0.7 all-gather.2.cloned.1.call-update
  7.3 0.9 fusion.16
  8.1 1.9 collective-permute-start
  10.1 12.4 %collective-permute-start.1 = (bf16[256,128]{1,0:T(8,128)(2,1)S(1)}, bf16[256,128]{1,0:T(8,128)(2,1)S(1)}, u32[]{:S(2)}, u32[]{:S(2)}) collective-permute-start(bf16[256,128]{1,0:T(8,128)(2,1)S(1)} %get-tuple-element.12), channel_id=1, source_target_pairs={{8,0},{16,8},{24,16},{32,24},{40,32},{48,40},{56,48},{64,56},{72,6... | collective-permute-start | bytes 196616 | tf_op jit(solution)/shard_map/ppermute | solution.py:19
  22.5 0.7 compare_select_fusion
  23.2 0.1 reshape.35
  23.3 0.0 collective-permute-done
  23.3 1.1 collective-permute-done.1
  24.4 1.0 pad_maximum_fusion
  25.3 0.9 gather_fusion
  26.3 42.6 %all-gather.2.cloned.1.call-done = bf16[8,7,128,128]{3,2,1,0:T(8,128)(2,1)} async-done(((bf16[8,7,16,128]{3,2,1,0:T(8,128)(2,1)}), bf16[8,7,128,128]{3,2,1,0:T(8,128)(2,1)}) %all-gather.2.cloned.1.call-update) | async-done | bytes 1835024 | tf_op jit(solution)/shard_map/all_gather | solution.py:36
  68.9 2.1 fusion.6
  71.0 3.2 collective-permute-start.3
  74.2 1.9 collective-permute-start.2
  76.2 0.0 collective-permute-done.3
  76.2 7.3 %collective-permute-done.2 = bf16[256,128]{1,0:T(8,128)(2,1)S(1)} collective-permute-done((bf16[256,128]{1,0:T(8,128)(2,1)S(1)}, bf16[256,128]{1,0:T(8,128)(2,1)S(1)}, u32[]{:S(2)}, u32[]{:S(2)}) %collective-permute-start.2) | collective-permute-done | bytes 65568 | tf_op jit(solution)/shard_map/ppermute | solution.py:16
  83.5 0.0 copy-start
  83.5 2.0 gather_fusion.1
  85.5 0.0 copy-done
  85.5 0.0 copy-start.1
  85.5 2.2 fusion.3
  87.7 0.0 copy-done.1
  87.7 0.1 fusion.10
  87.8 1.9 collective-permute-start.4
  89.7 7.3 %collective-permute-start.5 = (bf16[256,128]{1,0:T(8,128)(2,1)S(1)}, bf16[256,128]{1,0:T(8,128)(2,1)S(1)}, u32[]{:S(2)}, u32[]{:S(2)}) collective-permute-start(bf16[256,128]{1,0:T(8,128)(2,1)S(1)} %get-tuple-element.8), channel_id=1, source_target_pairs={{8,0},{16,8},{24,16},{32,24},{40,32},{48,40},{56,48},{64,56},{72,6... | collective-permute-start | bytes 196616 | tf_op jit(solution)/shard_map/ppermute | solution.py:19
  97.0 0.0 collective-permute-done.4
  97.0 1.9 collective-permute-done.5
  98.9 2.1 gather_fusion.2
  101.0 2.1 fusion.4
  103.1 0.1 fusion.9
  103.2 1.9 collective-permute-start.6
  105.1 7.3 %collective-permute-start.7 = (bf16[256,128]{1,0:T(8,128)(2,1)S(1)}, bf16[256,128]{1,0:T(8,128)(2,1)S(1)}, u32[]{:S(2)}, u32[]{:S(2)}) collective-permute-start(bf16[256,128]{1,0:T(8,128)(2,1)S(1)} %get-tuple-element.6), channel_id=1, source_target_pairs={{8,0},{16,8},{24,16},{32,24},{40,32},{48,40},{56,48},{64,56},{72,6... | collective-permute-start | bytes 196616 | tf_op jit(solution)/shard_map/ppermute | solution.py:19
  112.4 0.8 fusion.11
  113.2 6.0 all-to-all-start.1
  119.2 0.0 collective-permute-done.6
  119.2 0.0 collective-permute-done.7
  119.3 2.1 gather_fusion.3
  121.4 3.0 fusion.8
  124.3 1.0 all-to-all-done.1
  125.4 4.7 all-to-all-start
  130.0 0.0 all-reduce.2.cloned.1.call-start
  130.0 0.2 copy.7
  130.2 5.9 all-to-all-done
  136.2 2.7 fusion.17
  138.9 0.0 all-reduce.2.cloned.1.call-update
  138.9 0.1 copy.6
  139.0 491.1 %all-reduce.2.cloned.1.call-done = f32[1024,1024]{1,0:T(8,128)} async-done(((f32[1024,1024]{1,0:T(8,128)}), f32[1024,1024]{1,0:T(8,128)}) %all-reduce.2.cloned.1.call-update) | async-done | bytes 4194320 | tf_op jit(solution)/shard_map/psum | solution.py:55
  630.1 3.4 fusion.7
  (7 shorter events, 0.1 us)
Async XLA Ops:
  6.5 62.3 %all-gather.2.cloned.1.call-start = ((), (), s32[]{:S(2)}) async-start(), calls=%async_computation.2 | async-start | bytes 2064384 | tf_op jit(solution)/shard_map/all_gather | solution.py:36
  8.1 15.1 %collective-permute-start = (bf16[256,128]{1,0:T(8,128)(2,1)S(1)}, bf16[256,128]{1,0:T(8,128)(2,1)S(1)}, u32[]{:S(2)}, u32[]{:S(2)}) collective-permute-start(bf16[256,128]{1,0:T(8,128)(2,1)S(1)} %get-tuple-element.11), channel_id=1, source_target_pairs={{0,8},{8,16},{16,24},{24,32},{32,40},{40,48},{48,56},{56,64},{64,7... | collective-permute-start | bytes 196616 | tf_op jit(solution)/shard_map/ppermute | solution.py:16
  10.1 14.3 %collective-permute-start.1 = (bf16[256,128]{1,0:T(8,128)(2,1)S(1)}, bf16[256,128]{1,0:T(8,128)(2,1)S(1)}, u32[]{:S(2)}, u32[]{:S(2)}) collective-permute-start(bf16[256,128]{1,0:T(8,128)(2,1)S(1)} %get-tuple-element.12), channel_id=1, source_target_pairs={{8,0},{16,8},{24,16},{32,24},{40,32},{48,40},{56,48},{64,56},{72,6... | collective-permute-start | bytes 196616 | tf_op jit(solution)/shard_map/ppermute | solution.py:19
  71.0 5.2 collective-permute-start.3
  74.2 9.2 %collective-permute-start.2 = (bf16[256,128]{1,0:T(8,128)(2,1)S(1)}, bf16[256,128]{1,0:T(8,128)(2,1)S(1)}, u32[]{:S(2)}, u32[]{:S(2)}) collective-permute-start(bf16[256,128]{1,0:T(8,128)(2,1)S(1)} %bitcast.83), channel_id=1, source_target_pairs={{0,8},{8,16},{16,24},{24,32},{32,40},{40,48},{48,56},{56,64},{64,7... | collective-permute-start | bytes 196616 | tf_op jit(solution)/shard_map/ppermute | solution.py:16
  83.5 2.0 copy-start
  85.5 2.2 copy-start.1
  87.8 9.2 %collective-permute-start.4 = (bf16[256,128]{1,0:T(8,128)(2,1)S(1)}, bf16[256,128]{1,0:T(8,128)(2,1)S(1)}, u32[]{:S(2)}, u32[]{:S(2)}) collective-permute-start(bf16[256,128]{1,0:T(8,128)(2,1)S(1)} %get-tuple-element.7), channel_id=1, source_target_pairs={{0,8},{8,16},{16,24},{24,32},{32,40},{40,48},{48,56},{56,64},{64,7... | collective-permute-start | bytes 196616 | tf_op jit(solution)/shard_map/ppermute | solution.py:16
  89.7 9.1 %collective-permute-start.5 = (bf16[256,128]{1,0:T(8,128)(2,1)S(1)}, bf16[256,128]{1,0:T(8,128)(2,1)S(1)}, u32[]{:S(2)}, u32[]{:S(2)}) collective-permute-start(bf16[256,128]{1,0:T(8,128)(2,1)S(1)} %get-tuple-element.8), channel_id=1, source_target_pairs={{8,0},{16,8},{24,16},{32,24},{40,32},{48,40},{56,48},{64,56},{72,6... | collective-permute-start | bytes 196616 | tf_op jit(solution)/shard_map/ppermute | solution.py:19
  103.2 16.1 %collective-permute-start.6 = (bf16[256,128]{1,0:T(8,128)(2,1)S(1)}, bf16[256,128]{1,0:T(8,128)(2,1)S(1)}, u32[]{:S(2)}, u32[]{:S(2)}) collective-permute-start(bf16[256,128]{1,0:T(8,128)(2,1)S(1)} %get-tuple-element.5), channel_id=1, source_target_pairs={{0,8},{8,16},{16,24},{24,32},{32,40},{40,48},{48,56},{56,64},{64,7... | collective-permute-start | bytes 196616 | tf_op jit(solution)/shard_map/ppermute | solution.py:16
  105.1 14.1 %collective-permute-start.7 = (bf16[256,128]{1,0:T(8,128)(2,1)S(1)}, bf16[256,128]{1,0:T(8,128)(2,1)S(1)}, u32[]{:S(2)}, u32[]{:S(2)}) collective-permute-start(bf16[256,128]{1,0:T(8,128)(2,1)S(1)} %get-tuple-element.6), channel_id=1, source_target_pairs={{8,0},{16,8},{24,16},{32,24},{40,32},{48,40},{56,48},{64,56},{72,6... | collective-permute-start | bytes 196616 | tf_op jit(solution)/shard_map/ppermute | solution.py:19
  113.2 12.2 %all-to-all-start.1 = ((bf16[8,128,128]{2,1,0:T(8,128)(2,1)}), bf16[8,128,128]{2,1,0:T(8,128)(2,1)S(1)}, u32[]{:S(2)}, u32[]{:S(2)}) async-start(bf16[8,128,128]{2,1,0:T(8,128)(2,1)} %fusion.11), calls=%async_computation.1 | async-start | bytes 524288 | tf_op jit(solution)/shard_map/all_to_all | solution.py:49
  125.4 10.8 %all-to-all-start = ((bf16[8,128,128]{1,2,0:T(8,128)(2,1)}), bf16[8,128,128]{1,2,0:T(8,128)(2,1)S(1)}, u32[]{:S(2)}, u32[]{:S(2)}) async-start(bf16[8,128,128]{1,2,0:T(8,128)(2,1)} %fusion.8), calls=%async_computation | async-start | bytes 524288 | tf_op jit(solution)/shard_map/all_to_all | solution.py:50
  130.0 500.1 %all-reduce.2.cloned.1.call-start = ((), (), s32[]{:S(2)}) async-start(), calls=%async_computation.3 | async-start | bytes 8388608 | tf_op jit(solution)/shard_map/psum | solution.py:55
Sparse Core Ops, SparseCore 0:
  9.3 59.4 all-gather.1
  139.0 491.0 all-reduce.1
where the time goes:
time: 641 us; the launch traced here: 640 us
  waiting for transfers between devices  552 us (86%)
  starting transfers between devices  48.6 us (8%)
  matrix products  15.5 us (2%)
  between operations  13.6 us (2%)
  local copies, waits for them, and re-layouts  8.39 us (1%)
    psum x1, waiting for transfers between devices, body(): summed = lax.psum(partial_value, ('slab', 'band'))  491 us
    all_gather x1, waiting for transfers between devices, body(): full_tiles = lax.all_gather(hamiltonian, 'band', axis=2, tiled=True)  42.6 us
    ppermute x4, starting transfers between devices, padded(): lax.ppermute(lax.slice_in_dim(block, 0, width, axis=dim), axis, backward)  30.2 us
  transfers between devices with their start and end apart: 12, of which 7 were waited for; matrix products, arithmetic and copies ran while one was open for 2% of the time, Pallas kernels for 0%

commit v1 on v0

--- a/solution.py
+++ b/solution.py
@@ -3,6 +3,7 @@
 import jax.numpy as jnp
 from jax import lax
 from jax.sharding import PartitionSpec as P
+from jax.lax import psum
 
 FACE = 2
 
@@ -52,7 +53,8 @@
     partial_value = jnp.einsum(
         "rb,rc->bc", strip_third, strip_applied, preferred_element_type=jnp.float32
     )
-    summed = lax.psum(partial_value, ("slab", "band"))
+    r2 = psum(partial_value, "slab")
+    summed = psum(r2, "band")
     gram_full = (summed * gram_scale).astype(jnp.bfloat16)
     mixed = jnp.dot(strip_third, gram_full, preferred_element_type=jnp.float32)
     return (strip_applied.astype(jnp.float32) - mixed).astype(jnp.bfloat16)

time: 641 us -> 890 us (1.39)
  the two profiles are of different devices: /device:TPU:2 before, /device:TPU:1 now
where the time goes in v1:
time: 890 us; the launch traced here: 889 us
  waiting for transfers between devices  804 us (90%)
  starting transfers between devices  45.5 us (5%)
  matrix products  15.5 us (2%)
  between operations  13.3 us (1%)
    psum x1, waiting for transfers between devices, body(): r2 = psum(partial_value, 'slab')  546 us
    psum x1, waiting for transfers between devices, body(): summed = psum(r2, 'band')  199 us
    all_gather x1, waiting for transfers between devices, body(): full_tiles = lax.all_gather(hamiltonian, 'band', axis=2, tiled=True)  44.6 us
    ppermute x4, starting transfers between devices, padded(): lax.ppermute(lax.slice_in_dim(block, 0, width, axis=dim), axis, backward)  18.9 us
    ppermute x4, starting transfers between devices, padded(): lax.ppermute(lax.slice_in_dim(block, block.shape[dim] - width, None, axis...  18.2 us
  transfers between devices with their start and end apart: 13, of which 8 were waited for; matrix products, arithmetic and copies ran while one was open for 1% of the time, Pallas kernels for 0%

profile of v1, /device:TPU:1, one launch (start us, length us, event | category | flops | bytes accessed | tf_op | source)
XLA Modules:
  0.0 889.3 jit_solution(10123520747897578629)
XLA Ops:
  6.5 0.0 all-gather.2.cloned.1.call-start
  6.5 0.7 all-gather.2.cloned.1.call-update
  7.3 0.9 fusion.16
  8.1 6.0 collective-permute-start
  14.2 4.6 collective-permute-start.1
  18.8 0.7 compare_select_fusion
  19.5 0.1 reshape.35
  19.6 0.0 collective-permute-done
  19.6 1.7 collective-permute-done.1
  21.3 1.0 pad_maximum_fusion
  22.3 0.9 gather_fusion
  23.2 44.6 %all-gather.2.cloned.1.call-done = bf16[8,7,128,128]{3,2,1,0:T(8,128)(2,1)} async-done(((bf16[8,7,16,128]{3,2,1,0:T(8,128)(2,1)}), bf16[8,7,128,128]{3,2,1,0:T(8,128)(2,1)}) %all-gather.2.cloned.1.call-update) | async-done | bytes 1835024 | tf_op jit(solution)/shard_map/all_gather | solution.py:37
  67.7 2.1 fusion.6
  69.9 4.5 collective-permute-start.3
  74.4 4.4 collective-permute-start.2
  78.8 0.0 collective-permute-done.3
  78.8 1.3 collective-permute-done.2
  80.2 0.0 copy-start
  80.2 2.0 gather_fusion.1
  82.2 0.0 copy-done
  82.2 0.0 copy-start.1
  82.2 2.2 fusion.3
  84.4 0.0 copy-done.1
  84.4 0.1 fusion.10
  84.5 5.8 collective-permute-start.4
  90.3 3.9 collective-permute-start.5
  94.1 0.0 collective-permute-done.4
  94.1 3.2 collective-permute-done.5
  97.4 2.1 gather_fusion.2
  99.4 2.1 fusion.4
  101.6 0.1 fusion.9
  101.7 1.9 collective-permute-start.6
  103.6 5.9 collective-permute-start.7
  109.5 0.8 fusion.11
  110.3 4.2 all-to-all-start.1
  114.5 0.0 collective-permute-done.6
  114.5 0.0 collective-permute-done.7
  114.6 2.1 gather_fusion.3
  116.6 3.0 fusion.8
  119.6 1.0 all-to-all-done.1
  120.7 4.1 all-to-all-start
  124.8 0.0 all-reduce.3.cloned.1.call-start
  124.8 0.2 copy.7
  125.0 5.9 all-to-all-done
  130.9 2.7 fusion.17
  133.6 0.0 all-reduce.3.cloned.1.call-update
  133.6 0.0 all-reduce.5.cloned.1.call-start
  133.7 546.1 %all-reduce.3.cloned.1.call-done = f32[1024,1024]{1,0:T(8,128)} async-done(((f32[1024,1024]{1,0:T(8,128)}), f32[1024,1024]{1,0:T(8,128)}) %all-reduce.3.cloned.1.call-update) | async-done | bytes 4194320 | tf_op jit(solution)/shard_map/psum | solution.py:56
  679.8 0.0 all-reduce.5.cloned.1.call-update
  679.8 0.1 copy.6
  680.0 199.4 %all-reduce.5.cloned.1.call-done = f32[1024,1024]{1,0:T(8,128)} async-done(((f32[1024,1024]{1,0:T(8,128)}), f32[1024,1024]{1,0:T(8,128)}) %all-reduce.5.cloned.1.call-update) | async-done | bytes 4194320 | tf_op jit(solution)/shard_map/psum | solution.py:57
  879.4 3.4 fusion.7
  (7 shorter events, 0.1 us)
Async XLA Ops:
  6.5 61.2 %all-gather.2.cloned.1.call-start = ((), (), s32[]{:S(2)}) async-start(), calls=%async_computation.2 | async-start | bytes 2064384 | tf_op jit(solution)/shard_map/all_gather | solution.py:37
  8.1 11.5 %collective-permute-start = (bf16[256,128]{1,0:T(8,128)(2,1)S(1)}, bf16[256,128]{1,0:T(8,128)(2,1)S(1)}, u32[]{:S(2)}, u32[]{:S(2)}) collective-permute-start(bf16[256,128]{1,0:T(8,128)(2,1)S(1)} %get-tuple-element.11), channel_id=1, source_target_pairs={{0,8},{8,16},{16,24},{24,32},{32,40},{40,48},{48,56},{56,64},{64,7... | collective-permute-start | bytes 196616 | tf_op jit(solution)/shard_map/ppermute | solution.py:17
  14.2 7.1 collective-permute-start.1
  69.9 8.9 %collective-permute-start.3 = (bf16[256,128]{1,0:T(8,128)(2,1)S(1)}, bf16[256,128]{1,0:T(8,128)(2,1)S(1)}, u32[]{:S(2)}, u32[]{:S(2)}) collective-permute-start(bf16[256,128]{1,0:T(8,128)(2,1)S(1)} %bitcast.84), channel_id=1, source_target_pairs={{8,0},{16,8},{24,16},{32,24},{40,32},{48,40},{56,48},{64,56},{72,6... | collective-permute-start | bytes 196616 | tf_op jit(solution)/shard_map/ppermute | solution.py:20
  74.4 5.8 collective-permute-start.2
  80.2 2.0 copy-start
  82.2 2.2 copy-start.1
  84.5 9.7 %collective-permute-start.4 = (bf16[256,128]{1,0:T(8,128)(2,1)S(1)}, bf16[256,128]{1,0:T(8,128)(2,1)S(1)}, u32[]{:S(2)}, u32[]{:S(2)}) collective-permute-start(bf16[256,128]{1,0:T(8,128)(2,1)S(1)} %get-tuple-element.7), channel_id=1, source_target_pairs={{0,8},{8,16},{16,24},{24,32},{32,40},{40,48},{48,56},{56,64},{64,7... | collective-permute-start | bytes 196616 | tf_op jit(solution)/shard_map/ppermute | solution.py:17
  90.3 7.1 collective-permute-start.5
  101.7 12.9 %collective-permute-start.6 = (bf16[256,128]{1,0:T(8,128)(2,1)S(1)}, bf16[256,128]{1,0:T(8,128)(2,1)S(1)}, u32[]{:S(2)}, u32[]{:S(2)}) collective-permute-start(bf16[256,128]{1,0:T(8,128)(2,1)S(1)} %get-tuple-element.5), channel_id=1, source_target_pairs={{0,8},{8,16},{16,24},{24,32},{32,40},{40,48},{48,56},{56,64},{64,7... | collective-permute-start | bytes 196616 | tf_op jit(solution)/shard_map/ppermute | solution.py:17
  103.6 10.9 %collective-permute-start.7 = (bf16[256,128]{1,0:T(8,128)(2,1)S(1)}, bf16[256,128]{1,0:T(8,128)(2,1)S(1)}, u32[]{:S(2)}, u32[]{:S(2)}) collective-permute-start(bf16[256,128]{1,0:T(8,128)(2,1)S(1)} %get-tuple-element.6), channel_id=1, source_target_pairs={{8,0},{16,8},{24,16},{32,24},{40,32},{48,40},{56,48},{64,56},{72,6... | collective-permute-start | bytes 196616 | tf_op jit(solution)/shard_map/ppermute | solution.py:20
  110.3 10.3 %all-to-all-start.1 = ((bf16[8,128,128]{2,1,0:T(8,128)(2,1)}), bf16[8,128,128]{2,1,0:T(8,128)(2,1)S(1)}, u32[]{:S(2)}, u32[]{:S(2)}) async-start(bf16[8,128,128]{2,1,0:T(8,128)(2,1)} %fusion.11), calls=%async_computation.1 | async-start | bytes 524288 | tf_op jit(solution)/shard_map/all_to_all | solution.py:50
  120.7 10.2 %all-to-all-start = ((bf16[8,128,128]{1,2,0:T(8,128)(2,1)}), bf16[8,128,128]{1,2,0:T(8,128)(2,1)S(1)}, u32[]{:S(2)}, u32[]{:S(2)}) async-start(bf16[8,128,128]{1,2,0:T(8,128)(2,1)} %fusion.8), calls=%async_computation | async-start | bytes 524288 | tf_op jit(solution)/shard_map/all_to_all | solution.py:51
  124.8 555.0 %all-reduce.3.cloned.1.call-start = ((), (), s32[]{:S(2)}) async-start(), calls=%async_computation.3 | async-start | bytes 8388608 | tf_op jit(solution)/shard_map/psum | solution.py:56
  133.6 745.8 %all-reduce.5.cloned.1.call-start = ((), (), s32[]{:S(2)}) async-start(), calls=%async_computation.4 | async-start | bytes 8388608 | tf_op jit(solution)/shard_map/psum | solution.py:57
Sparse Core Ops, SparseCore 0:
  9.3 58.3 all-gather.1
  133.7 546.0 all-reduce.2
  682.8 196.5 all-reduce.4
